TPU v7x, 256 devices: a whole 4x4x8 slice. The times are simulated.
256 devices in a mesh: section: 8 (over y, core), dp: 32 (over z, x).
Axes of the slice: x: 4, y: 4, z: 8, core: 2. Of those that a mesh axis runs over, the one named last changes fastest.
Arguments:
- crop_maps: bfloat16 [32, 4, 2, 8, 8, 640], P('dp'), may hold values from -6 to 6
- target_maps: int32 [32, 4, 2, 8, 8], P('dp'), may hold values 0 or 1
- crop_counts: int32 [32, 4], P('dp'), may hold values from 1 to 2, as said below
- depth_kernels: float32 [8, 49, 640], P('section'), may hold values from -0.875 to 0.875
- weight_in: bfloat16 [8, 640, 2560], P('section', 'dp'), may hold values from -0.25 to 0.25
- weight_out: bfloat16 [8, 2560, 640], P('section', 'dp'), may hold values from -0.125 to 0.125
- head_weight: float32 [640], replicated, may hold values from -0.25 to 0.25
Outputs:
- grad_in: float32 [8, 640, 2560], P('section', 'dp')
- grad_out: float32 [8, 2560, 640], P('section', 'dp')
- grad_kernels: float32 [8, 49, 640], P('section')
- grad_head: float32 [640], replicated
- loss_value: float32 [], replicated
Inputs may be any that keep to these rules, and one draw needn't show every extreme that they name: `crop_counts`: every data group has some micro-batch with exactly 2 crops.
All inputs are finite; a program needn't handle non-finite values. No bound on the sum of `target_maps` on one device may be relied on, other than what follows from the above.
Results may differ from a plain program's by a relative error of at most 0.034.
Values may be sent and summed in bfloat16 or wider, within the bound.
No kernel may reach another device: no remote copies, remote signals or barrier semaphores. Data moves between devices by JAX's collectives and lax.ppermute only.
A program may use at most 128 MiB of HBM per device.

v0:
```python
import jax
import jax.numpy as jnp
from jax import lax
from jax.sharding import PartitionSpec as P

EPSILON = 1e-06
SQRT_HALF = 0.7071067811865476
INV_ROOT_TWO_PI = 0.3989422804014327


def from_behind(value, axis, steps):
    count = lax.axis_size(axis)
    first, last = (max(0, -steps), min(count, count - steps))
    return lax.ppermute(value, axis, [(source, source + steps) for source in range(first, last)])


def depthwise(values, kernel):
    side = values.shape[1]
    padded = jnp.pad(values, ((0, 0), (3, 3), (3, 3), (0, 0)))
    result = jnp.zeros_like(values)
    for vertical in range(7):
        for across in range(7):
            result = (
                result
                + padded[:, vertical : vertical + side, across : across + side, :]
                * kernel[vertical * 7 + across]
            )
    return result


def depthwise_back(grads, kernel):
    side = grads.shape[1]
    padded = jnp.pad(grads, ((0, 0), (3, 3), (3, 3), (0, 0)))
    result = jnp.zeros_like(grads)
    for vertical in range(7):
        for across in range(7):
            result = (
                result
                + padded[:, 6 - vertical : 6 - vertical + side, 6 - across : 6 - across + side, :]
                * kernel[vertical * 7 + across]
            )
    return result


def kernel_grad(values, grads):
    side = values.shape[1]
    padded = jnp.pad(values, ((0, 0), (3, 3), (3, 3), (0, 0)))
    taps = []
    for vertical in range(7):
        for across in range(7):
            taps.append(
                jnp.sum(
                    padded[:, vertical : vertical + side, across : across + side, :] * grads,
                    axis=(0, 1, 2),
                )
            )
    return jnp.stack(taps, axis=0)


def block_parts(tiles, kernel, weight_in):
    width = tiles.shape[-1]
    widened = tiles.astype(jnp.float32)
    mixed = depthwise(widened, kernel).reshape(-1, width)
    centred = mixed - jnp.mean(mixed, axis=-1, keepdims=True)
    inverse = lax.rsqrt(jnp.mean(centred * centred, axis=-1, keepdims=True) + EPSILON)
    normed = centred * inverse
    normed_low = normed.astype(jnp.bfloat16)
    hidden = jnp.dot(normed_low, weight_in, preferred_element_type=jnp.float32)
    activated = (hidden * 0.5 * (1.0 + lax.erf(hidden * SQRT_HALF))).astype(jnp.bfloat16)
    return (widened, normed, inverse, normed_low, hidden, activated)


def block_forward(tiles, kernel, weight_in, weight_out):
    width = tiles.shape[-1]
    widened, normed, inverse, normed_low, hidden, activated = block_parts(tiles, kernel, weight_in)
    output = jnp.dot(activated, weight_out, preferred_element_type=jnp.float32)
    return (widened.reshape(-1, width) + output).astype(jnp.bfloat16).reshape(tiles.shape)


def block_backward(tiles, upstream, kernel, weight_in, weight_out):
    width = tiles.shape[-1]
    widened, normed, inverse, normed_low, hidden, activated = block_parts(tiles, kernel, weight_in)
    up_flat = upstream.reshape(-1, width)
    through = lax.dot_general(
        up_flat, weight_out, (((1,), (1,)), ((), ())), preferred_element_type=jnp.float32
    )
    slope = (
        0.5 * (1.0 + lax.erf(hidden * SQRT_HALF))
        + hidden * jnp.exp(-0.5 * hidden * hidden) * INV_ROOT_TWO_PI
    )
    hidden_grad = (through * slope).astype(jnp.bfloat16)
    normed_grad = lax.dot_general(
        hidden_grad, weight_in, (((1,), (1,)), ((), ())), preferred_element_type=jnp.float32
    )
    mixed_grad = inverse * (
        normed_grad
        - jnp.mean(normed_grad, axis=-1, keepdims=True)
        - normed * jnp.mean(normed_grad * normed, axis=-1, keepdims=True)
    )
    mixed_tiles = mixed_grad.reshape(tiles.shape)
    kernel_term = kernel_grad(widened, mixed_tiles)
    tile_grad = (upstream.astype(jnp.float32) + depthwise_back(mixed_tiles, kernel)).astype(
        jnp.bfloat16
    )
    return (tile_grad, kernel_term, normed_low, hidden_grad, activated, up_flat)


def outer_sum(left, right):
    return lax.dot_general(
        left, right, (((0,), (0,)), ((), ())), preferred_element_type=jnp.float32
    )


def head_terms(final, targets, live, head_weight, factor):
    widened = final.astype(jnp.float32)
    logits = jnp.sum(widened * head_weight, axis=-1)
    weight_live = live.astype(jnp.float32)[:, :, None, None]
    truth = targets.astype(jnp.float32)
    loss_term = jnp.sum(weight_live * (jax.nn.softplus(logits) - truth * logits)) * factor
    logit_grad = (jax.nn.sigmoid(logits) - truth) * weight_live * factor
    seeds = (logit_grad[..., None] * head_weight).astype(jnp.bfloat16)
    head_term = jnp.sum(logit_grad[..., None] * widened, axis=(0, 1, 2, 3))
    return (loss_term, seeds, head_term)


def body(crop_maps, target_maps, crop_counts, depth_kernels, weight_in, weight_out, head_weight):
    section_index = lax.axis_index("section")
    section_count = lax.axis_size("section")
    micro_count = crop_maps.shape[1]
    slot_count = crop_maps.shape[2]
    kernel = depth_kernels[0]
    live = jnp.arange(slot_count)[None, :] < crop_counts[0][:, None]
    entering = crop_maps[0] * live[:, :, None, None, None].astype(jnp.bfloat16)
    first_full, second_full = (
        lax.all_gather(weight_in[0], "dp", axis=0, tiled=True),
        lax.all_gather(weight_out[0], "dp", axis=0, tiled=True),
    )
    blank_tile = jnp.zeros(entering.shape[1:], jnp.bfloat16)
    ticks = micro_count + section_count - 1

    def forward_step(moment, carry):
        arrived, saved, final = carry
        micro = moment - section_index
        active = (micro >= 0) & (micro < micro_count)
        place = jnp.clip(micro, 0, micro_count - 1)
        own_tiles = lax.dynamic_index_in_dim(entering, place, 0, keepdims=False)
        current = jnp.where(section_index == 0, own_tiles, arrived)
        result = lax.cond(
            active,
            lambda tiles: block_forward(tiles, kernel, first_full, second_full),
            lambda tiles: jnp.zeros_like(tiles),
            current,
        )
        old_saved = lax.dynamic_index_in_dim(saved, place, 0, keepdims=False)
        saved = lax.dynamic_update_index_in_dim(
            saved, jnp.where(active, current, old_saved), place, 0
        )
        old_final = lax.dynamic_index_in_dim(final, place, 0, keepdims=False)
        final = lax.dynamic_update_index_in_dim(
            final, jnp.where(active, result, old_final), place, 0
        )
        arrived = from_behind(result, "section", 1)
        return (arrived, saved, final)

    _, saved, final = lax.fori_loop(
        0, ticks, forward_step, (blank_tile, jnp.zeros_like(entering), jnp.zeros_like(entering))
    )
    is_last = section_index == section_count - 1
    last_weight = is_last.astype(jnp.float32)
    factor = 1.0 / (micro_count * slot_count)
    loss_term, seeds, head_term = head_terms(final, target_maps[0], live, head_weight, factor)
    head_total, loss_total = lax.psum(
        (head_term * last_weight, loss_term * last_weight), ("section", "dp")
    )
    first_back, second_back = (
        lax.all_gather(weight_in[0], "dp", axis=0, tiled=True),
        lax.all_gather(weight_out[0], "dp", axis=0, tiled=True),
    )
    width = entering.shape[-1]
    expand = first_back.shape[1]
    extra_start = (jnp.zeros((width, expand), jnp.float32), jnp.zeros((expand, width), jnp.float32))

    def backward_step(moment, carry):
        arrived, kernel_acc, extra = carry
        micro = moment - (section_count - 1 - section_index)
        active = (micro >= 0) & (micro < micro_count)
        place = jnp.clip(micro, 0, micro_count - 1)
        own_seed = lax.dynamic_index_in_dim(seeds, place, 0, keepdims=False)
        upstream = jnp.where(is_last, own_seed, arrived)
        stored = lax.dynamic_index_in_dim(saved, place, 0, keepdims=False)

        def run_block(operands):
            grad_tiles, inputs, acc_kernel, acc_extra = operands
            tile_grad, kernel_term, normed_low, hidden_grad, activated, up_flat = block_backward(
                inputs, grad_tiles, kernel, first_back, second_back
            )
            new_extra = (
                acc_extra[0] + outer_sum(normed_low, hidden_grad),
                acc_extra[1] + outer_sum(activated, up_flat),
            )
            return (tile_grad, acc_kernel + kernel_term, new_extra)

        def skip_block(operands):
            return (jnp.zeros_like(operands[0]), operands[2], operands[3])

        tile_grad, kernel_acc, extra = lax.cond(
            active, run_block, skip_block, (upstream, stored, kernel_acc, extra)
        )
        arrived = from_behind(tile_grad, "section", -1)
        return (arrived, kernel_acc, extra)

    _, kernel_acc, extra = lax.fori_loop(
        0, ticks, backward_step, (blank_tile, jnp.zeros(kernel.shape, jnp.float32), extra_start)
    )
    first_part, second_part = (
        lax.psum_scatter(
            extra[0].astype(jnp.bfloat16), "dp", scatter_dimension=0, tiled=True
        ).astype(jnp.float32),
        lax.psum_scatter(
            extra[1].astype(jnp.bfloat16), "dp", scatter_dimension=0, tiled=True
        ).astype(jnp.float32),
    )
    kernel_total = lax.psum(kernel_acc.astype(jnp.bfloat16), "dp").astype(jnp.float32)
    return (first_part[None], second_part[None], kernel_total[None], head_total, loss_total)


def solution(mesh):
    return jax.shard_map(
        body,
        mesh=mesh,
        in_specs=(
            P("dp", None, None, None, None, None),
            P("dp", None, None, None, None),
            P("dp", None),
            P("section", None, None),
            P("section", "dp", None),
            P("section", "dp", None),
            P(),
        ),
        out_specs=(
            P("section", "dp", None),
            P("section", "dp", None),
            P("section", None, None),
            P(),
            P(),
        ),
        check_vma=False,
    )
```

profile of v0, /device:TPU:1, one launch (start us, length us, event | category | flops | bytes accessed | tf_op | source)
XLA Modules:
  0.0 1533.0 jit_solution(5656709828315738469)
XLA Ops:
  13.1 91.3 %all-gather.5.cloned.1.call-done = bf16[1,640,2560]{2,0,1:T(2,128)(2,1)} async-done(((bf16[1,20,2560]{2,0,1:T(2,128)(2,1)}), bf16[1,640,2560]{2,0,1:T(2,128)(2,1)}) %all-gather.5.cloned.1.call-update) | async-done | bytes 3276816 | tf_op jit(solution)/shard_map/all_gather | solution.py:135
  104.4 3.6 copy.20
  108.0 72.7 %all-gather.7.cloned.1.call-done = bf16[1,2560,640]{2,1,0:T(8,128)(2,1)} async-done(((bf16[1,80,640]{2,1,0:T(8,128)(2,1)}), bf16[1,2560,640]{2,1,0:T(8,128)(2,1)}) %all-gather.7.cloned.1.call-update) | async-done | bytes 3276816 | tf_op jit(solution)/shard_map/all_gather | solution.py:136
  183.2 210.7 %while.40 = (s32[]{:T(128)}, bf16[2,8,8,640]{3,2,1,0:T(8,128)(2,1)}, bf16[4,2,8,8,640]{4,3,2,1,0:T(8,128)(2,1)}, bf16[4,2,8,8,640]{4,3,2,1,0:T(8,128)(2,1)}, s32...) while((s32[]{:T(128)}, ...), condition=%wide.region_5.6_spmd, body=%wide.region_0.5_spmd.sunk | while | flops 849510528 | bytes 13491009 | solution.py:165
  185.9 7.7 collective-permute-start
  195.4 12.2 collective-permute-done
  210.3 14.7 conditional.5
  215.8 2.9 fusion.228
  221.8 3.3 fusion.3
  231.9 14.7 conditional.5
  237.4 2.9 fusion.228
  243.4 3.3 fusion.3
  246.6 4.5 collective-permute-start
  256.1 14.7 conditional.5
  261.6 2.9 fusion.228
  267.5 3.3 fusion.3
  270.8 4.5 collective-permute-start
  280.3 14.7 conditional.5
  285.8 2.9 fusion.228
  291.7 3.3 fusion.3
  295.0 4.5 collective-permute-start
  304.5 19.2 %collective-permute-start = (bf16[2,8,8,640]{3,2,1,0:T(8,128)(2,1)S(1)}, bf16[2,8,8,640]{3,2,1,0:T(8,128)(2,1)}, u32[]{:S(2)}, u32[]{:S(2)}) collective-permute-start(bf16[2,8,8,640]{3,2,1,0:T(8,128)(2,1)S(1)} %get-tuple-element.1153), channel_id=1, source_target_pairs={{0,32},{32,64},{64,96},{96,128},{128,160},{160,192},{192,224},{1,3... | collective-permute-start | bytes 491528 | tf_op jit(solution)/shard_map/while/body/eval_jaxpr/ppermute | solution.py:14
  328.7 4.5 collective-permute-start
  338.2 12.7 collective-permute-start
  355.9 4.5 collective-permute-start
  365.5 16.6 %collective-permute-start = (bf16[2,8,8,640]{3,2,1,0:T(8,128)(2,1)S(1)}, bf16[2,8,8,640]{3,2,1,0:T(8,128)(2,1)}, u32[]{:S(2)}, u32[]{:S(2)}) collective-permute-start(bf16[2,8,8,640]{3,2,1,0:T(8,128)(2,1)S(1)} %get-tuple-element.1153), channel_id=1, source_target_pairs={{0,32},{32,64},{64,96},{96,128},{128,160},{160,192},{192,224},{1,3... | collective-permute-start | bytes 491528 | tf_op jit(solution)/shard_map/while/body/eval_jaxpr/ppermute | solution.py:14
  387.1 4.5 collective-permute-start
  396.5 3.1 broadcast_in_dim.59
  399.7 3.5 broadcast_in_dim.58
  403.2 778.2 %while.41 = (s32[]{:T(128)}, bf16[2,8,8,640]{3,2,1,0:T(8,128)(2,1)}, f32[49,640]{1,0:T(8,128)S(1)}, f32[640,2560]{1,0:T(8,128)}, f32[2560,640]{1,0:T(8,128)}, /*...) while((s32[]{:T(128)}, ...), condition=%wide.region_63.64_spmd.clone, body=%wide.region_7.63_spmd.clone.sunk | while | flops 2131804288 | bytes 130983528 | solution.py:212
  407.5 14.1 collective-permute-done.1
  425.9 5.0 collective-permute-done.1
  435.2 17.3 %collective-permute-done.1 = bf16[2,8,8,640]{3,2,1,0:T(8,128)(2,1)} collective-permute-done((bf16[2,8,8,640]{3,2,1,0:T(8,128)(2,1)}, bf16[2,8,8,640]{3,2,1,0:T(8,128)(2,1)}, u32[]{:S(2)}, u32[]{:S(2)}) %collective-permute-start.1) | collective-permute-done | bytes 163872 | tf_op jit(solution)/shard_map/while/body/eval_jaxpr/ppermute | solution.py:14
  456.8 5.0 collective-permute-done.1
  466.1 13.4 collective-permute-done.1
  483.8 359.0 %collective-permute-done.1 = bf16[2,8,8,640]{3,2,1,0:T(8,128)(2,1)} collective-permute-done((bf16[2,8,8,640]{3,2,1,0:T(8,128)(2,1)}, bf16[2,8,8,640]{3,2,1,0:T(8,128)(2,1)}, u32[]{:S(2)}, u32[]{:S(2)}) %collective-permute-start.1) | collective-permute-done | bytes 163872 | tf_op jit(solution)/shard_map/while/body/eval_jaxpr/ppermute | solution.py:14
  844.6 60.5 %conditional.6 = (bf16[2,8,8,640]{3,2,1,0:T(8,128)(2,1)}, f32[49,640]{1,0:T(8,128)S(1)}, f32[640,2560]{1,0:T(8,128)}, f32[2560,640]{1,0:T(8,128)}) conditional(s32[]{:T(128)} %convert_element_type.175, (f32[49,640]{1,0:T(8,128)S(1)}, f32[640,2560]{1,0:T(8,128)}, f32[2560,640]{1,0:T(8,128)}) %tuple.251, (pred[]{:T(512)}, s32[]{:T(128)}, ...), branch_computations={%region_8.8_spmd, %region_9.62_spmd} | conditional | flops 2131148928 | bytes 129667864 | solution.py:206
  848.7 2.9 fusion.230
  884.0 8.0 stack.299
  893.8 7.2 convolution_add_fusion.1
  902.3 2.7 copy-done
  906.9 5.0 collective-permute-done.1
  913.7 60.5 %conditional.6 = (bf16[2,8,8,640]{3,2,1,0:T(8,128)(2,1)}, f32[49,640]{1,0:T(8,128)S(1)}, f32[640,2560]{1,0:T(8,128)}, f32[2560,640]{1,0:T(8,128)}) conditional(s32[]{:T(128)} %convert_element_type.175, (f32[49,640]{1,0:T(8,128)S(1)}, f32[640,2560]{1,0:T(8,128)}, f32[2560,640]{1,0:T(8,128)}) %tuple.251, (pred[]{:T(512)}, s32[]{:T(128)}, ...), branch_computations={%region_8.8_spmd, %region_9.62_spmd} | conditional | flops 2131148928 | bytes 129667864 | solution.py:206
  917.8 2.9 fusion.230
  953.1 8.0 stack.299
  962.9 7.2 convolution_add_fusion.1
  976.0 5.0 collective-permute-done.1
  982.8 60.5 %conditional.6 = (bf16[2,8,8,640]{3,2,1,0:T(8,128)(2,1)}, f32[49,640]{1,0:T(8,128)S(1)}, f32[640,2560]{1,0:T(8,128)}, f32[2560,640]{1,0:T(8,128)}) conditional(s32[]{:T(128)} %convert_element_type.175, (f32[49,640]{1,0:T(8,128)S(1)}, f32[640,2560]{1,0:T(8,128)}, f32[2560,640]{1,0:T(8,128)}) %tuple.251, (pred[]{:T(512)}, s32[]{:T(128)}, ...), branch_computations={%region_8.8_spmd, %region_9.62_spmd} | conditional | flops 2131148928 | bytes 129667864 | solution.py:206
  986.9 2.9 fusion.230
  1022.2 8.0 stack.299
  1032.0 7.2 convolution_add_fusion.1
  1045.1 5.0 collective-permute-done.1
  1051.9 60.5 %conditional.6 = (bf16[2,8,8,640]{3,2,1,0:T(8,128)(2,1)}, f32[49,640]{1,0:T(8,128)S(1)}, f32[640,2560]{1,0:T(8,128)}, f32[2560,640]{1,0:T(8,128)}) conditional(s32[]{:T(128)} %convert_element_type.175, (f32[49,640]{1,0:T(8,128)S(1)}, f32[640,2560]{1,0:T(8,128)}, f32[2560,640]{1,0:T(8,128)}) %tuple.251, (pred[]{:T(512)}, s32[]{:T(128)}, ...), branch_computations={%region_8.8_spmd, %region_9.62_spmd} | conditional | flops 2131148928 | bytes 129667864 | solution.py:206
  1056.0 2.9 fusion.230
  1091.3 8.0 stack.299
  1101.1 7.2 convolution_add_fusion.1
  1114.2 5.0 collective-permute-done.1
  1121.6 58.4 %collective-permute-start.1 = (bf16[2,8,8,640]{3,2,1,0:T(8,128)(2,1)}, bf16[2,8,8,640]{3,2,1,0:T(8,128)(2,1)}, u32[]{:S(2)}, u32[]{:S(2)}) collective-permute-start(bf16[2,8,8,640]{3,2,1,0:T(8,128)(2,1)} %get-tuple-element.1051), channel_id=1, source_target_pairs={{32,0},{64,32},{96,64},{128,96},{160,128},{192,160},{224,192},{33,... | collective-permute-start | bytes 491528 | tf_op jit(solution)/shard_map/while/body/eval_jaxpr/ppermute | solution.py:14
  1181.3 4.9 convert_element_type.134
  1188.1 3.2 convert_element_type.133
  1191.4 84.2 %fusion.2 = bf16[24,2560]{1,0:T(8,128)(2,1)} fusion(bf16[640,2560]{1,0:T(8,128)(2,1)S(1)} %convert_element_type.133), kind=kCustom, calls=%all-reduce-scatter | all-reduce-scatter fusion | flops 1966081 | bytes 3400704
  1283.4 9.5 collective-permute-start.7
  1294.3 110.5 %psum.21 = bf16[1,49,640]{2,0,1:T(2,128)(2,1)S(1)} all-reduce(bf16[1,49,640]{2,0,1:T(2,128)(2,1)S(1)} %broadcast_in_dim.64), channel_id=1, replica_groups=mesh['section'=8,'dp'=32] {'dp'}, use_global_device_ids=true, to_apply=%region_66.67 | all-reduce | flops 31360 | bytes 125440 | tf_op jit(solution)/shard_map/psum | solution.py:223
  1406.9 115.7 %all-reduce.5 = (f32[640]{0:T(1024)}, f32[]{:T(128)}) all-reduce(f32[640]{0:T(1024)S(1)} %broadcast_multiply_fusion.4, f32[]{:T(128)S(6)} %mul.2377), channel_id=1, replica_groups=mesh['section'=8,'dp'=32] {'section','dp'}, use_global_device_ids=true, to_apply=%region_68.69 | all-reduce | flops 641 | bytes 5128 | tf_op jit(solution)/shard_map/psum | solution.py:172
  (1136 shorter events, 327.4 us)
Async XLA Ops:
  7.2 5.0 copy-start.76
  7.2 97.2 %all-gather.5.cloned.1.call-start = ((), (), s32[]{:S(2)}) async-start(), calls=%async_computation.2 | async-start | bytes 6758400 | tf_op jit(solution)/shard_map/all_gather | solution.py:135
  9.0 171.6 %all-gather.7.cloned.1.call-start = ((), (), s32[]{:S(2)}) async-start(), calls=%async_computation.3 | async-start | bytes 3379200 | tf_op jit(solution)/shard_map/all_gather | solution.py:136
  9.8 1515.1 %reduce-scatter.4.cloned.1.call-start = ((), (), s32[]{:S(2)}) async-start(), calls=%async_computation.1 | async-start | bytes 3379200 | tf_op jit(solution)/shard_map/reduce_scatter | solution.py:219
  183.2 212.0 %copy-start.81 = (s32[1,4,2,8,8]{4,3,2,1,0:T(8,128)S(1)}, s32[1,4,2,8,8]{4,3,2,1,0:T(8,128)}, u32[]{:S(2)}) copy-start(s32[1,4,2,8,8]{4,3,2,1,0:T(8,128)} %param.16) | copy-start | bytes 6148
  185.9 21.6 %collective-permute-start = (bf16[2,8,8,640]{3,2,1,0:T(8,128)(2,1)S(1)}, bf16[2,8,8,640]{3,2,1,0:T(8,128)(2,1)}, u32[]{:S(2)}, u32[]{:S(2)}) collective-permute-start(bf16[2,8,8,640]{3,2,1,0:T(8,128)(2,1)S(1)} %get-tuple-element.1153), channel_id=1, source_target_pairs={{0,32},{32,64},{64,96},{96,128},{128,160},{160,192},{192,224},{1,3... | collective-permute-start | bytes 491528 | tf_op jit(solution)/shard_map/while/body/eval_jaxpr/ppermute | solution.py:14
  225.0 4.2 collective-permute-start
  246.6 6.8 collective-permute-start
  270.8 6.7 collective-permute-start
  295.0 6.7 collective-permute-start
  304.5 21.4 %collective-permute-start = (bf16[2,8,8,640]{3,2,1,0:T(8,128)(2,1)S(1)}, bf16[2,8,8,640]{3,2,1,0:T(8,128)(2,1)}, u32[]{:S(2)}, u32[]{:S(2)}) collective-permute-start(bf16[2,8,8,640]{3,2,1,0:T(8,128)(2,1)S(1)} %get-tuple-element.1153), channel_id=1, source_target_pairs={{0,32},{32,64},{64,96},{96,128},{128,160},{160,192},{192,224},{1,3... | collective-permute-start | bytes 491528 | tf_op jit(solution)/shard_map/while/body/eval_jaxpr/ppermute | solution.py:14
  328.7 6.7 collective-permute-start
  338.2 14.9 collective-permute-start
  355.9 6.7 collective-permute-start
  365.5 18.8 %collective-permute-start = (bf16[2,8,8,640]{3,2,1,0:T(8,128)(2,1)S(1)}, bf16[2,8,8,640]{3,2,1,0:T(8,128)(2,1)}, u32[]{:S(2)}, u32[]{:S(2)}) collective-permute-start(bf16[2,8,8,640]{3,2,1,0:T(8,128)(2,1)S(1)} %get-tuple-element.1153), channel_id=1, source_target_pairs={{0,32},{32,64},{64,96},{96,128},{128,160},{160,192},{192,224},{1,3... | collective-permute-start | bytes 491528 | tf_op jit(solution)/shard_map/while/body/eval_jaxpr/ppermute | solution.py:14
  387.1 6.7 collective-permute-start
  405.6 16.0 %collective-permute-start.1 = (bf16[2,8,8,640]{3,2,1,0:T(8,128)(2,1)}, bf16[2,8,8,640]{3,2,1,0:T(8,128)(2,1)}, u32[]{:S(2)}, u32[]{:S(2)}) collective-permute-start(bf16[2,8,8,640]{3,2,1,0:T(8,128)(2,1)} %get-tuple-element.1051), channel_id=1, source_target_pairs={{32,0},{64,32},{96,64},{128,96},{160,128},{192,160},{224,192},{33,... | collective-permute-start | bytes 491528 | tf_op jit(solution)/shard_map/while/body/eval_jaxpr/ppermute | solution.py:14
  423.9 6.9 collective-permute-start.1
  433.3 19.2 %collective-permute-start.1 = (bf16[2,8,8,640]{3,2,1,0:T(8,128)(2,1)}, bf16[2,8,8,640]{3,2,1,0:T(8,128)(2,1)}, u32[]{:S(2)}, u32[]{:S(2)}) collective-permute-start(bf16[2,8,8,640]{3,2,1,0:T(8,128)(2,1)} %get-tuple-element.1051), channel_id=1, source_target_pairs={{32,0},{64,32},{96,64},{128,96},{160,128},{192,160},{224,192},{33,... | collective-permute-start | bytes 491528 | tf_op jit(solution)/shard_map/while/body/eval_jaxpr/ppermute | solution.py:14
  454.9 6.9 collective-permute-start.1
  464.2 15.3 %collective-permute-start.1 = (bf16[2,8,8,640]{3,2,1,0:T(8,128)(2,1)}, bf16[2,8,8,640]{3,2,1,0:T(8,128)(2,1)}, u32[]{:S(2)}, u32[]{:S(2)}) collective-permute-start(bf16[2,8,8,640]{3,2,1,0:T(8,128)(2,1)} %get-tuple-element.1051), channel_id=1, source_target_pairs={{32,0},{64,32},{96,64},{128,96},{160,128},{192,160},{224,192},{33,... | collective-permute-start | bytes 491528 | tf_op jit(solution)/shard_map/while/body/eval_jaxpr/ppermute | solution.py:14
  481.9 361.0 %collective-permute-start.1 = (bf16[2,8,8,640]{3,2,1,0:T(8,128)(2,1)}, bf16[2,8,8,640]{3,2,1,0:T(8,128)(2,1)}, u32[]{:S(2)}, u32[]{:S(2)}) collective-permute-start(bf16[2,8,8,640]{3,2,1,0:T(8,128)(2,1)} %get-tuple-element.1051), channel_id=1, source_target_pairs={{32,0},{64,32},{96,64},{128,96},{160,128},{192,160},{224,192},{33,... | collective-permute-start | bytes 491528 | tf_op jit(solution)/shard_map/while/body/eval_jaxpr/ppermute | solution.py:14
  848.2 3.5 copy-start.14
  860.9 3.7 copy-start.3
  864.6 19.4 %copy-start.78 = (f32[1,640]{1,0:T(1,128)S(1)}, f32[1,640]{1,0:T(1,128)}, u32[]{:S(2)}) copy-start(f32[1,640]{1,0:T(1,128)} %stack.274) | copy-start | bytes 7684 | tf_op jit(solution)/shard_map/while/body/eval_jaxpr/cond
  892.0 9.0 slice-start
  893.8 7.2 slice-start.1
  893.8 7.2 copy-start.6
  893.8 7.2 copy-start.8
  901.0 4.1 copy-start.13
  905.0 6.9 collective-permute-start.1
  930.0 3.7 copy-start.3
  933.7 19.4 %copy-start.78 = (f32[1,640]{1,0:T(1,128)S(1)}, f32[1,640]{1,0:T(1,128)}, u32[]{:S(2)}) copy-start(f32[1,640]{1,0:T(1,128)} %stack.274) | copy-start | bytes 7684 | tf_op jit(solution)/shard_map/while/body/eval_jaxpr/cond
  961.1 9.0 slice-start
  962.9 7.2 slice-start.1
  962.9 7.2 copy-start.6
  962.9 7.2 copy-start.8
  970.1 4.1 copy-start.13
  974.1 6.9 collective-permute-start.1
  986.4 3.5 copy-start.14
  999.1 3.7 copy-start.3
  1002.8 19.4 %copy-start.78 = (f32[1,640]{1,0:T(1,128)S(1)}, f32[1,640]{1,0:T(1,128)}, u32[]{:S(2)}) copy-start(f32[1,640]{1,0:T(1,128)} %stack.274) | copy-start | bytes 7684 | tf_op jit(solution)/shard_map/while/body/eval_jaxpr/cond
  1030.2 9.0 slice-start
  1032.0 7.2 slice-start.1
  1032.0 7.2 copy-start.6
  1032.0 7.2 copy-start.8
  1039.1 4.1 copy-start.13
  1043.2 6.9 collective-permute-start.1
  1068.2 3.7 copy-start.3
  1071.9 19.4 %copy-start.78 = (f32[1,640]{1,0:T(1,128)S(1)}, f32[1,640]{1,0:T(1,128)}, u32[]{:S(2)}) copy-start(f32[1,640]{1,0:T(1,128)} %stack.274) | copy-start | bytes 7684 | tf_op jit(solution)/shard_map/while/body/eval_jaxpr/cond
  1099.2 9.0 slice-start
  1101.0 7.2 slice-start.1
  1101.0 7.2 copy-start.6
  1101.1 7.2 copy-start.8
  1108.2 4.1 copy-start.13
  1112.3 6.9 collective-permute-start.1
  1121.6 59.7 %collective-permute-start.1 = (bf16[2,8,8,640]{3,2,1,0:T(8,128)(2,1)}, bf16[2,8,8,640]{3,2,1,0:T(8,128)(2,1)}, u32[]{:S(2)}, u32[]{:S(2)}) collective-permute-start(bf16[2,8,8,640]{3,2,1,0:T(8,128)(2,1)} %get-tuple-element.1051), channel_id=1, source_target_pairs={{32,0},{64,32},{96,64},{128,96},{160,128},{192,160},{224,192},{33,... | collective-permute-start | bytes 491528 | tf_op jit(solution)/shard_map/while/body/eval_jaxpr/ppermute | solution.py:14
  1275.6 130.0 %copy-start.77 = (bf16[24,2560]{1,0:T(8,128)(2,1)S(1)}, bf16[24,2560]{1,0:T(8,128)(2,1)}, u32[]{:S(2)}) copy-start(bf16[24,2560]{1,0:T(8,128)(2,1)} %fusion.2) | copy-start | bytes 368644
  1276.5 246.1 %collective-permute-start.6 = (bf16[24,2560]{1,0:T(8,128)(2,1)}, bf16[24,2560]{1,0:T(8,128)(2,1)S(1)}, u32[]{:S(2)}, u32[]{:S(2)}) collective-permute-start(bf16[24,2560]{1,0:T(8,128)(2,1)} %fusion.2), channel_id=1, source_target_pairs={{0,5},{1,6},{2,7},{3,8},{4,9},{5,10},{6,11},{7,12},{8,13},{9,14},{... | collective-permute-start | bytes 368648
  1277.8 244.8 %collective-permute-start.5 = (bf16[24,2560]{1,0:T(8,128)(2,1)}, bf16[24,2560]{1,0:T(8,128)(2,1)S(1)}, u32[]{:S(2)}, u32[]{:S(2)}) collective-permute-start(bf16[24,2560]{1,0:T(8,128)(2,1)} %fusion.2), channel_id=1, source_target_pairs={{0,4},{1,5},{2,6},{3,7},{4,8},{5,9},{6,10},{7,11},{8,12},{9,13},{1... | collective-permute-start | bytes 368648
  1279.3 243.3 %collective-permute-start.4 = (bf16[24,2560]{1,0:T(8,128)(2,1)}, bf16[24,2560]{1,0:T(8,128)(2,1)S(1)}, u32[]{:S(2)}, u32[]{:S(2)}) collective-permute-start(bf16[24,2560]{1,0:T(8,128)(2,1)} %fusion.2), channel_id=1, source_target_pairs={{0,3},{1,4},{2,5},{3,6},{4,7},{5,8},{6,9},{7,10},{8,11},{9,12},{10... | collective-permute-start | bytes 368648
  1280.6 242.0 %collective-permute-start.3 = (bf16[24,2560]{1,0:T(8,128)(2,1)}, bf16[24,2560]{1,0:T(8,128)(2,1)S(1)}, u32[]{:S(2)}, u32[]{:S(2)}) collective-permute-start(bf16[24,2560]{1,0:T(8,128)(2,1)} %fusion.2), channel_id=1, source_target_pairs={{0,2},{1,3},{2,4},{3,5},{4,6},{5,7},{6,8},{7,9},{8,10},{9,11},{10,... | collective-permute-start | bytes 368648
  1283.4 122.2 %collective-permute-start.7 = (bf16[4,2560]{1,0:T(4,128)(2,1)S(1)}, bf16[4,2560]{1,0:T(4,128)(2,1)S(1)}, u32[]{:S(2)}, u32[]{:S(2)}) collective-permute-start(bf16[4,2560]{1,0:T(4,128)(2,1)S(1)} %slice.1262), channel_id=1, source_target_pairs={{0,6},{1,7},{2,8},{3,9},{4,10},{5,11},{6,12},{7,13},{8,14},{9,15},... | collective-permute-start | bytes 61448
  1405.6 117.0 %collective-permute-start.2 = (bf16[24,2560]{1,0:T(8,128)(2,1)S(1)}, bf16[24,2560]{1,0:T(8,128)(2,1)S(1)}, u32[]{:S(2)}, u32[]{:S(2)}) collective-permute-start(bf16[24,2560]{1,0:T(8,128)(2,1)S(1)} %copy-done.77), channel_id=1, source_target_pairs={{0,1},{1,2},{2,3},{3,4},{4,5},{5,6},{6,7},{7,8},{8,9},{9,10},{10,1... | collective-permute-start | bytes 368648
  (299 other events, 619.8 us)
Sparse Core Ops, SparseCore 0:
  11.2 93.1 all-gather.4
  107.0 73.6 all-gather.6
  1186.4 193.5 reduce-scatter.3
where the time goes:
time: 1540 us; the launch traced here: 1530 us
  waiting for transfers between devices  618 us (40%)
  blocking collectives  310 us (20%)
  local copies, waits for them, and re-layouts  199 us (13%)
  starting transfers between devices  180 us (12%)
  other arithmetic  145 us (9%)
  matrix products  59.4 us (4%)
    ppermute x22, waiting for transfers between devices, from_behind(): lax.ppermute(value, axis, [(source, source + steps) for source in range(f...  453 us
    ppermute x22, starting transfers between devices, from_behind(): lax.ppermute(value, axis, [(source, source + steps) for source in range(f...  163 us
    psum x1, blocking collectives, body(): lax.psum((head_term * last_weight, loss_term * last_weight), ('section',...  116 us
    psum x1, blocking collectives, body(): lax.psum(kernel_acc.astype(jnp.bfloat16), 'dp').astype(jnp.float32)  111 us
    another operation x200, local copies, waits for them, and re-layouts, kernel_grad(): return jnp.stack(taps, axis=0)  105 us
    all_gather x1, waiting for transfers between devices, body(): lax.all_gather(weight_in[0], 'dp', axis=0, tiled=True)  91.3 us
    unnamed x1, blocking collectives  84.2 us
    all_gather x1, waiting for transfers between devices, body(): lax.all_gather(weight_out[0], 'dp', axis=0, tiled=True)  72.7 us
  transfers between devices with their start and end apart: 31, of which 24 were waited for; matrix products, arithmetic and copies ran while one was open for 8% of the time, Pallas kernels for 0%

commit v1 on v0

--- a/solution.py
+++ b/solution.py
@@ -220,7 +220,9 @@
             extra[1].astype(jnp.bfloat16), "dp", scatter_dimension=0, tiled=True
         ).astype(jnp.float32),
     )
-    kernel_total = lax.psum(kernel_acc.astype(jnp.bfloat16), "dp").astype(jnp.float32)
+    kernel_total = jnp.sum(lax.all_gather(kernel_acc.astype(jnp.bfloat16), "dp"), axis=0).astype(
+        jnp.float32
+    )
     return (first_part[None], second_part[None], kernel_total[None], head_total, loss_total)
 
 

time: 1540 us -> 1470 us (0.955)
  blocking collectives: 310 us -> 167 us
  waiting for transfers between devices: 618 us -> 687 us
    psum x1 -> x0, blocking collectives: 111 us -> none  [body(): lax.psum(kernel_acc.astype(jnp.bfloat16), 'dp').astype(jnp.float32)]
    reduce_scatter x1, waiting for transfers between devices: 0.01 us -> 69 us  [body(): lax.psum_scatter(extra[1].astype(jnp.bfloat16), 'dp', scatter_dimension=0...]
    psum x1, blocking collectives: 116 us -> 85.4 us  [body(): lax.psum((head_term * last_weight, loss_term * last_weight), ('section',...]
  transfers between devices with their start and end apart: 31 -> 32, of which waited for: 24 -> 25; matrix products, arithmetic and copies ran while one was open for 8% -> 8% of each run, Pallas kernels for 0% -> 0%
where the time goes in v1:
time: 1470 us; the launch traced here: 1460 us
  waiting for transfers between devices  687 us (47%)
  local copies, waits for them, and re-layouts  199 us (14%)
  starting transfers between devices  183 us (12%)
  blocking collectives  167 us (11%)
  other arithmetic  147 us (10%)
  matrix products  59.4 us (4%)
  between operations  15.2 us (1%)
    ppermute x22, waiting for transfers between devices, from_behind(): lax.ppermute(value, axis, [(source, source + steps) for source in range(f...  453 us
    ppermute x22, starting transfers between devices, from_behind(): lax.ppermute(value, axis, [(source, source + steps) for source in range(f...  163 us
    another operation x200, local copies, waits for them, and re-layouts, kernel_grad(): return jnp.stack(taps, axis=0)  105 us
    all_gather x1, waiting for transfers between devices, body(): lax.all_gather(weight_in[0], 'dp', axis=0, tiled=True)  91.3 us
    psum x1, blocking collectives, body(): lax.psum((head_term * last_weight, loss_term * last_weight), ('section',...  85.4 us
    unnamed x1, blocking collectives  81.5 us
    all_gather x1, waiting for transfers between devices, body(): lax.all_gather(weight_out[0], 'dp', axis=0, tiled=True)  72.7 us
    reduce_scatter x1, waiting for transfers between devices, body(): lax.psum_scatter(extra[1].astype(jnp.bfloat16), 'dp', scatter_dimension=0...  69 us
  transfers between devices with their start and end apart: 32, of which 25 were waited for; matrix products, arithmetic and copies ran while one was open for 8% of the time, Pallas kernels for 0%

profile of v1, /device:TPU:1, one launch (start us, length us, event | category | flops | bytes accessed | tf_op | source)
XLA Modules:
  0.0 1463.8 jit_solution(2081399517478236099)
XLA Ops:
  13.1 91.3 %all-gather.8.cloned.1.call-done = bf16[1,640,2560]{2,0,1:T(2,128)(2,1)} async-done(((bf16[1,20,2560]{2,0,1:T(2,128)(2,1)}), bf16[1,640,2560]{2,0,1:T(2,128)(2,1)}) %all-gather.8.cloned.1.call-update) | async-done | bytes 3276816 | tf_op jit(solution)/shard_map/all_gather | solution.py:135
  104.4 3.6 copy.20
  108.0 72.7 %all-gather.10.cloned.1.call-done = bf16[1,2560,640]{2,1,0:T(8,128)(2,1)} async-done(((bf16[1,80,640]{2,1,0:T(8,128)(2,1)}), bf16[1,2560,640]{2,1,0:T(8,128)(2,1)}) %all-gather.10.cloned.1.call-update) | async-done | bytes 3276816 | tf_op jit(solution)/shard_map/all_gather | solution.py:136
  183.2 210.7 %while.40 = (s32[]{:T(128)}, bf16[2,8,8,640]{3,2,1,0:T(8,128)(2,1)}, bf16[4,2,8,8,640]{4,3,2,1,0:T(8,128)(2,1)}, bf16[4,2,8,8,640]{4,3,2,1,0:T(8,128)(2,1)}, s32...) while((s32[]{:T(128)}, ...), condition=%wide.region_5.6_spmd, body=%wide.region_0.5_spmd.sunk | while | flops 849510528 | bytes 13491009 | solution.py:165
  185.9 7.7 collective-permute-start
  195.4 12.2 collective-permute-done
  210.3 14.7 %conditional.5 = (bf16[2,8,8,640]{3,2,1,0:T(8,128)(2,1)S(1)}) conditional(s32[]{:T(128)} %convert_element_type.191, () %tuple.248, (bf16[2,8,8,640]{3,2,1,0:T(8,128)(2,1)}, f32[49,640]{1,0:T(8,128)}, bf16[640,2560]{1,0:T(8,128)(2,1)S(1)}, bf16[2560,640]{1,0:T(8,128)(2,1)}) %tuple.249), branch_computations={%region_1.1_spmd, %region_2.4_spmd} | conditional | flops 849264768 | bytes 10868772 | solution.py:148
  215.8 2.9 fusion.228
  221.8 3.3 fusion.3
  231.9 14.7 %conditional.5 = (bf16[2,8,8,640]{3,2,1,0:T(8,128)(2,1)S(1)}) conditional(s32[]{:T(128)} %convert_element_type.191, () %tuple.248, (bf16[2,8,8,640]{3,2,1,0:T(8,128)(2,1)}, f32[49,640]{1,0:T(8,128)}, bf16[640,2560]{1,0:T(8,128)(2,1)S(1)}, bf16[2560,640]{1,0:T(8,128)(2,1)}) %tuple.249), branch_computations={%region_1.1_spmd, %region_2.4_spmd} | conditional | flops 849264768 | bytes 10868772 | solution.py:148
  237.4 2.9 fusion.228
  243.4 3.3 fusion.3
  246.6 4.5 collective-permute-start
  256.1 14.7 %conditional.5 = (bf16[2,8,8,640]{3,2,1,0:T(8,128)(2,1)S(1)}) conditional(s32[]{:T(128)} %convert_element_type.191, () %tuple.248, (bf16[2,8,8,640]{3,2,1,0:T(8,128)(2,1)}, f32[49,640]{1,0:T(8,128)}, bf16[640,2560]{1,0:T(8,128)(2,1)S(1)}, bf16[2560,640]{1,0:T(8,128)(2,1)}) %tuple.249), branch_computations={%region_1.1_spmd, %region_2.4_spmd} | conditional | flops 849264768 | bytes 10868772 | solution.py:148
  261.6 2.9 fusion.228
  267.5 3.3 fusion.3
  270.8 4.5 collective-permute-start
  280.3 14.7 %conditional.5 = (bf16[2,8,8,640]{3,2,1,0:T(8,128)(2,1)S(1)}) conditional(s32[]{:T(128)} %convert_element_type.191, () %tuple.248, (bf16[2,8,8,640]{3,2,1,0:T(8,128)(2,1)}, f32[49,640]{1,0:T(8,128)}, bf16[640,2560]{1,0:T(8,128)(2,1)S(1)}, bf16[2560,640]{1,0:T(8,128)(2,1)}) %tuple.249), branch_computations={%region_1.1_spmd, %region_2.4_spmd} | conditional | flops 849264768 | bytes 10868772 | solution.py:148
  291.7 3.3 fusion.3
  295.0 4.5 collective-permute-start
  304.5 19.2 %collective-permute-start = (bf16[2,8,8,640]{3,2,1,0:T(8,128)(2,1)S(1)}, bf16[2,8,8,640]{3,2,1,0:T(8,128)(2,1)}, u32[]{:S(2)}, u32[]{:S(2)}) collective-permute-start(bf16[2,8,8,640]{3,2,1,0:T(8,128)(2,1)S(1)} %get-tuple-element.1153), channel_id=1, source_target_pairs={{0,32},{32,64},{64,96},{96,128},{128,160},{160,192},{192,224},{1,3... | collective-permute-start | bytes 491528 | tf_op jit(solution)/shard_map/while/body/eval_jaxpr/ppermute | solution.py:14
  328.7 4.5 collective-permute-start
  338.2 12.7 collective-permute-start
  355.9 4.5 collective-permute-start
  365.5 16.6 %collective-permute-start = (bf16[2,8,8,640]{3,2,1,0:T(8,128)(2,1)S(1)}, bf16[2,8,8,640]{3,2,1,0:T(8,128)(2,1)}, u32[]{:S(2)}, u32[]{:S(2)}) collective-permute-start(bf16[2,8,8,640]{3,2,1,0:T(8,128)(2,1)S(1)} %get-tuple-element.1153), channel_id=1, source_target_pairs={{0,32},{32,64},{64,96},{96,128},{128,160},{160,192},{192,224},{1,3... | collective-permute-start | bytes 491528 | tf_op jit(solution)/shard_map/while/body/eval_jaxpr/ppermute | solution.py:14
  387.1 4.5 collective-permute-start
  396.5 3.1 broadcast_in_dim.54
  399.7 3.5 broadcast_in_dim.53
  403.2 778.2 %while.41 = (s32[]{:T(128)}, bf16[2,8,8,640]{3,2,1,0:T(8,128)(2,1)}, f32[49,640]{1,0:T(8,128)S(1)}, f32[640,2560]{1,0:T(8,128)}, f32[2560,640]{1,0:T(8,128)}, /*...) while((s32[]{:T(128)}, ...), condition=%wide.region_63.64_spmd.clone, body=%wide.region_7.63_spmd.clone.sunk | while | flops 2131804288 | bytes 130983528 | solution.py:212
  407.5 14.1 collective-permute-done.1
  425.9 5.0 collective-permute-done.1
  435.2 17.3 %collective-permute-done.1 = bf16[2,8,8,640]{3,2,1,0:T(8,128)(2,1)} collective-permute-done((bf16[2,8,8,640]{3,2,1,0:T(8,128)(2,1)}, bf16[2,8,8,640]{3,2,1,0:T(8,128)(2,1)}, u32[]{:S(2)}, u32[]{:S(2)}) %collective-permute-start.1) | collective-permute-done | bytes 163872 | tf_op jit(solution)/shard_map/while/body/eval_jaxpr/ppermute | solution.py:14
  456.8 5.0 collective-permute-done.1
  466.1 13.4 collective-permute-done.1
  483.8 359.0 %collective-permute-done.1 = bf16[2,8,8,640]{3,2,1,0:T(8,128)(2,1)} collective-permute-done((bf16[2,8,8,640]{3,2,1,0:T(8,128)(2,1)}, bf16[2,8,8,640]{3,2,1,0:T(8,128)(2,1)}, u32[]{:S(2)}, u32[]{:S(2)}) %collective-permute-start.1) | collective-permute-done | bytes 163872 | tf_op jit(solution)/shard_map/while/body/eval_jaxpr/ppermute | solution.py:14
  844.6 60.5 %conditional.6 = (bf16[2,8,8,640]{3,2,1,0:T(8,128)(2,1)}, f32[49,640]{1,0:T(8,128)S(1)}, f32[640,2560]{1,0:T(8,128)}, f32[2560,640]{1,0:T(8,128)}) conditional(s32[]{:T(128)} %convert_element_type.193, (f32[49,640]{1,0:T(8,128)S(1)}, f32[640,2560]{1,0:T(8,128)}, f32[2560,640]{1,0:T(8,128)}) %tuple.251, (pred[]{:T(512)}, s32[]{:T(128)}, ...), branch_computations={%region_8.8_spmd, %region_9.62_spmd} | conditional | flops 2131148928 | bytes 129667864 | solution.py:206
  848.7 2.9 fusion.230
  884.0 8.0 stack.299
  893.8 7.2 convolution_add_fusion.1
  906.9 5.0 collective-permute-done.1
  913.7 60.5 %conditional.6 = (bf16[2,8,8,640]{3,2,1,0:T(8,128)(2,1)}, f32[49,640]{1,0:T(8,128)S(1)}, f32[640,2560]{1,0:T(8,128)}, f32[2560,640]{1,0:T(8,128)}) conditional(s32[]{:T(128)} %convert_element_type.193, (f32[49,640]{1,0:T(8,128)S(1)}, f32[640,2560]{1,0:T(8,128)}, f32[2560,640]{1,0:T(8,128)}) %tuple.251, (pred[]{:T(512)}, s32[]{:T(128)}, ...), branch_computations={%region_8.8_spmd, %region_9.62_spmd} | conditional | flops 2131148928 | bytes 129667864 | solution.py:206
  917.8 2.9 fusion.230
  953.1 8.0 stack.299
  962.9 7.2 convolution_add_fusion.1
  976.0 5.0 collective-permute-done.1
  982.8 60.5 %conditional.6 = (bf16[2,8,8,640]{3,2,1,0:T(8,128)(2,1)}, f32[49,640]{1,0:T(8,128)S(1)}, f32[640,2560]{1,0:T(8,128)}, f32[2560,640]{1,0:T(8,128)}) conditional(s32[]{:T(128)} %convert_element_type.193, (f32[49,640]{1,0:T(8,128)S(1)}, f32[640,2560]{1,0:T(8,128)}, f32[2560,640]{1,0:T(8,128)}) %tuple.251, (pred[]{:T(512)}, s32[]{:T(128)}, ...), branch_computations={%region_8.8_spmd, %region_9.62_spmd} | conditional | flops 2131148928 | bytes 129667864 | solution.py:206
  986.9 2.9 fusion.230
  1022.2 8.0 stack.299
  1032.0 7.2 convolution_add_fusion.1
  1045.1 5.0 collective-permute-done.1
  1051.9 60.5 %conditional.6 = (bf16[2,8,8,640]{3,2,1,0:T(8,128)(2,1)}, f32[49,640]{1,0:T(8,128)S(1)}, f32[640,2560]{1,0:T(8,128)}, f32[2560,640]{1,0:T(8,128)}) conditional(s32[]{:T(128)} %convert_element_type.193, (f32[49,640]{1,0:T(8,128)S(1)}, f32[640,2560]{1,0:T(8,128)}, f32[2560,640]{1,0:T(8,128)}) %tuple.251, (pred[]{:T(512)}, s32[]{:T(128)}, ...), branch_computations={%region_8.8_spmd, %region_9.62_spmd} | conditional | flops 2131148928 | bytes 129667864 | solution.py:206
  1056.0 2.9 fusion.230
  1091.3 8.0 stack.299
  1101.1 7.2 convolution_add_fusion.1
  1114.2 5.0 collective-permute-done.1
  1121.6 58.4 %collective-permute-start.1 = (bf16[2,8,8,640]{3,2,1,0:T(8,128)(2,1)}, bf16[2,8,8,640]{3,2,1,0:T(8,128)(2,1)}, u32[]{:S(2)}, u32[]{:S(2)}) collective-permute-start(bf16[2,8,8,640]{3,2,1,0:T(8,128)(2,1)} %get-tuple-element.1051), channel_id=1, source_target_pairs={{32,0},{64,32},{96,64},{128,96},{160,128},{192,160},{224,192},{33,... | collective-permute-start | bytes 491528 | tf_op jit(solution)/shard_map/while/body/eval_jaxpr/ppermute | solution.py:14
  1182.1 4.9 convert_element_type.148
  1188.8 3.2 convert_element_type.147
  1192.1 81.5 %fusion.2 = bf16[24,2560]{1,0:T(8,128)(2,1)S(1)} fusion(bf16[640,2560]{1,0:T(8,128)(2,1)S(1)} %convert_element_type.147), kind=kCustom, calls=%all-reduce-scatter | all-reduce-scatter fusion | flops 1966081 | bytes 3400704
  1277.7 6.0 collective-permute-start.5
  1283.8 4.6 collective-permute-start.4
  1288.4 5.6 collective-permute-start.3
  1296.2 85.4 %all-reduce.5 = (f32[640]{0:T(1024)}, f32[]{:T(128)}) all-reduce(f32[640]{0:T(1024)S(1)} %broadcast_multiply_fusion.4, f32[]{:T(128)S(6)} %mul.2377), channel_id=1, replica_groups=mesh['section'=8,'dp'=32] {'section','dp'}, use_global_device_ids=true, to_apply=%region_68.69 | all-reduce | flops 641 | bytes 5128 | tf_op jit(solution)/shard_map/psum | solution.py:172
  1386.7 69.0 %reduce-scatter.4.cloned.1.call-done = bf16[80,640]{1,0:T(8,128)(2,1)} async-done(((bf16[2560,640]{1,0:T(8,128)(2,1)}), bf16[80,640]{1,0:T(8,128)(2,1)}) %reduce-scatter.4.cloned.1.call-update) | async-done | bytes 102416 | tf_op jit(solution)/shard_map/reduce_scatter | solution.py:219
  (1136 shorter events, 331.5 us)
Async XLA Ops:
  7.2 5.0 copy-start.76
  7.2 97.2 %all-gather.8.cloned.1.call-start = ((), (), s32[]{:S(2)}) async-start(), calls=%async_computation.2 | async-start | bytes 6758400 | tf_op jit(solution)/shard_map/all_gather | solution.py:135
  9.0 171.6 %all-gather.10.cloned.1.call-start = ((), (), s32[]{:S(2)}) async-start(), calls=%async_computation.3 | async-start | bytes 3379200 | tf_op jit(solution)/shard_map/all_gather | solution.py:136
  9.8 1374.2 %all-gather.12.cloned.1.call-start = ((), (), s32[]{:S(2)}) async-start(), calls=%async_computation.4 | async-start | bytes 2365440 | tf_op jit(solution)/shard_map/all_gather | solution.py:223
  183.2 212.0 %copy-start.80 = (s32[1,4,2,8,8]{4,3,2,1,0:T(8,128)S(1)}, s32[1,4,2,8,8]{4,3,2,1,0:T(8,128)}, u32[]{:S(2)}) copy-start(s32[1,4,2,8,8]{4,3,2,1,0:T(8,128)} %param.16) | copy-start | bytes 6148
  185.9 21.6 %collective-permute-start = (bf16[2,8,8,640]{3,2,1,0:T(8,128)(2,1)S(1)}, bf16[2,8,8,640]{3,2,1,0:T(8,128)(2,1)}, u32[]{:S(2)}, u32[]{:S(2)}) collective-permute-start(bf16[2,8,8,640]{3,2,1,0:T(8,128)(2,1)S(1)} %get-tuple-element.1153), channel_id=1, source_target_pairs={{0,32},{32,64},{64,96},{96,128},{128,160},{160,192},{192,224},{1,3... | collective-permute-start | bytes 491528 | tf_op jit(solution)/shard_map/while/body/eval_jaxpr/ppermute | solution.py:14
  225.0 4.2 collective-permute-start
  246.6 6.8 collective-permute-start
  270.8 6.7 collective-permute-start
  295.0 6.7 collective-permute-start
  304.5 21.4 %collective-permute-start = (bf16[2,8,8,640]{3,2,1,0:T(8,128)(2,1)S(1)}, bf16[2,8,8,640]{3,2,1,0:T(8,128)(2,1)}, u32[]{:S(2)}, u32[]{:S(2)}) collective-permute-start(bf16[2,8,8,640]{3,2,1,0:T(8,128)(2,1)S(1)} %get-tuple-element.1153), channel_id=1, source_target_pairs={{0,32},{32,64},{64,96},{96,128},{128,160},{160,192},{192,224},{1,3... | collective-permute-start | bytes 491528 | tf_op jit(solution)/shard_map/while/body/eval_jaxpr/ppermute | solution.py:14
  328.7 6.7 collective-permute-start
  338.2 14.9 %collective-permute-start = (bf16[2,8,8,640]{3,2,1,0:T(8,128)(2,1)S(1)}, bf16[2,8,8,640]{3,2,1,0:T(8,128)(2,1)}, u32[]{:S(2)}, u32[]{:S(2)}) collective-permute-start(bf16[2,8,8,640]{3,2,1,0:T(8,128)(2,1)S(1)} %get-tuple-element.1153), channel_id=1, source_target_pairs={{0,32},{32,64},{64,96},{96,128},{128,160},{160,192},{192,224},{1,3... | collective-permute-start | bytes 491528 | tf_op jit(solution)/shard_map/while/body/eval_jaxpr/ppermute | solution.py:14
  355.9 6.7 collective-permute-start
  365.5 18.8 %collective-permute-start = (bf16[2,8,8,640]{3,2,1,0:T(8,128)(2,1)S(1)}, bf16[2,8,8,640]{3,2,1,0:T(8,128)(2,1)}, u32[]{:S(2)}, u32[]{:S(2)}) collective-permute-start(bf16[2,8,8,640]{3,2,1,0:T(8,128)(2,1)S(1)} %get-tuple-element.1153), channel_id=1, source_target_pairs={{0,32},{32,64},{64,96},{96,128},{128,160},{160,192},{192,224},{1,3... | collective-permute-start | bytes 491528 | tf_op jit(solution)/shard_map/while/body/eval_jaxpr/ppermute | solution.py:14
  387.1 6.7 collective-permute-start
  405.6 16.0 %collective-permute-start.1 = (bf16[2,8,8,640]{3,2,1,0:T(8,128)(2,1)}, bf16[2,8,8,640]{3,2,1,0:T(8,128)(2,1)}, u32[]{:S(2)}, u32[]{:S(2)}) collective-permute-start(bf16[2,8,8,640]{3,2,1,0:T(8,128)(2,1)} %get-tuple-element.1051), channel_id=1, source_target_pairs={{32,0},{64,32},{96,64},{128,96},{160,128},{192,160},{224,192},{33,... | collective-permute-start | bytes 491528 | tf_op jit(solution)/shard_map/while/body/eval_jaxpr/ppermute | solution.py:14
  423.9 6.9 collective-permute-start.1
  433.3 19.2 %collective-permute-start.1 = (bf16[2,8,8,640]{3,2,1,0:T(8,128)(2,1)}, bf16[2,8,8,640]{3,2,1,0:T(8,128)(2,1)}, u32[]{:S(2)}, u32[]{:S(2)}) collective-permute-start(bf16[2,8,8,640]{3,2,1,0:T(8,128)(2,1)} %get-tuple-element.1051), channel_id=1, source_target_pairs={{32,0},{64,32},{96,64},{128,96},{160,128},{192,160},{224,192},{33,... | collective-permute-start | bytes 491528 | tf_op jit(solution)/shard_map/while/body/eval_jaxpr/ppermute | solution.py:14
  454.9 6.9 collective-permute-start.1
  464.2 15.3 %collective-permute-start.1 = (bf16[2,8,8,640]{3,2,1,0:T(8,128)(2,1)}, bf16[2,8,8,640]{3,2,1,0:T(8,128)(2,1)}, u32[]{:S(2)}, u32[]{:S(2)}) collective-permute-start(bf16[2,8,8,640]{3,2,1,0:T(8,128)(2,1)} %get-tuple-element.1051), channel_id=1, source_target_pairs={{32,0},{64,32},{96,64},{128,96},{160,128},{192,160},{224,192},{33,... | collective-permute-start | bytes 491528 | tf_op jit(solution)/shard_map/while/body/eval_jaxpr/ppermute | solution.py:14
  481.9 361.0 %collective-permute-start.1 = (bf16[2,8,8,640]{3,2,1,0:T(8,128)(2,1)}, bf16[2,8,8,640]{3,2,1,0:T(8,128)(2,1)}, u32[]{:S(2)}, u32[]{:S(2)}) collective-permute-start(bf16[2,8,8,640]{3,2,1,0:T(8,128)(2,1)} %get-tuple-element.1051), channel_id=1, source_target_pairs={{32,0},{64,32},{96,64},{128,96},{160,128},{192,160},{224,192},{33,... | collective-permute-start | bytes 491528 | tf_op jit(solution)/shard_map/while/body/eval_jaxpr/ppermute | solution.py:14
  848.2 3.5 copy-start.14
  860.9 3.7 copy-start.3
  864.6 19.4 %copy-start.77 = (f32[1,640]{1,0:T(1,128)S(1)}, f32[1,640]{1,0:T(1,128)}, u32[]{:S(2)}) copy-start(f32[1,640]{1,0:T(1,128)} %stack.274) | copy-start | bytes 7684 | tf_op jit(solution)/shard_map/while/body/eval_jaxpr/cond
  892.0 9.0 slice-start
  893.8 7.2 slice-start.1
  893.8 7.2 copy-start.6
  893.8 7.2 copy-start.8
  901.0 4.1 copy-start.13
  905.0 6.9 collective-permute-start.1
  930.0 3.7 copy-start.3
  933.7 19.4 %copy-start.77 = (f32[1,640]{1,0:T(1,128)S(1)}, f32[1,640]{1,0:T(1,128)}, u32[]{:S(2)}) copy-start(f32[1,640]{1,0:T(1,128)} %stack.274) | copy-start | bytes 7684 | tf_op jit(solution)/shard_map/while/body/eval_jaxpr/cond
  961.1 9.0 slice-start
  962.9 7.2 slice-start.1
  962.9 7.2 copy-start.6
  962.9 7.2 copy-start.8
  970.1 4.1 copy-start.13
  974.1 6.9 collective-permute-start.1
  986.4 3.5 copy-start.14
  999.1 3.7 copy-start.3
  1002.8 19.4 %copy-start.77 = (f32[1,640]{1,0:T(1,128)S(1)}, f32[1,640]{1,0:T(1,128)}, u32[]{:S(2)}) copy-start(f32[1,640]{1,0:T(1,128)} %stack.274) | copy-start | bytes 7684 | tf_op jit(solution)/shard_map/while/body/eval_jaxpr/cond
  1030.2 9.0 slice-start
  1032.0 7.2 slice-start.1
  1032.0 7.2 copy-start.6
  1032.0 7.2 copy-start.8
  1039.1 4.1 copy-start.13
  1043.2 6.9 collective-permute-start.1
  1068.2 3.7 copy-start.3
  1071.9 19.4 %copy-start.77 = (f32[1,640]{1,0:T(1,128)S(1)}, f32[1,640]{1,0:T(1,128)}, u32[]{:S(2)}) copy-start(f32[1,640]{1,0:T(1,128)} %stack.274) | copy-start | bytes 7684 | tf_op jit(solution)/shard_map/while/body/eval_jaxpr/cond
  1099.2 9.0 slice-start
  1101.0 7.2 slice-start.1
  1101.0 7.2 copy-start.6
  1101.1 7.2 copy-start.8
  1108.2 4.1 copy-start.13
  1112.3 6.9 collective-permute-start.1
  1121.6 59.7 %collective-permute-start.1 = (bf16[2,8,8,640]{3,2,1,0:T(8,128)(2,1)}, bf16[2,8,8,640]{3,2,1,0:T(8,128)(2,1)}, u32[]{:S(2)}, u32[]{:S(2)}) collective-permute-start(bf16[2,8,8,640]{3,2,1,0:T(8,128)(2,1)} %get-tuple-element.1051), channel_id=1, source_target_pairs={{32,0},{64,32},{96,64},{128,96},{160,128},{192,160},{224,192},{33,... | collective-permute-start | bytes 491528 | tf_op jit(solution)/shard_map/while/body/eval_jaxpr/ppermute | solution.py:14
  1182.0 273.6 %reduce-scatter.4.cloned.1.call-start = ((), (), s32[]{:S(2)}) async-start(), calls=%async_computation.1 | async-start | bytes 3379200 | tf_op jit(solution)/shard_map/reduce_scatter | solution.py:219
  1273.6 21.0 %collective-permute-start.7 = (bf16[4,2560]{1,0:T(4,128)(2,1)S(1)}, bf16[4,2560]{1,0:T(4,128)(2,1)S(1)}, u32[]{:S(2)}, u32[]{:S(2)}) collective-permute-start(bf16[4,2560]{1,0:T(4,128)(2,1)S(1)} %slice.1262), channel_id=1, source_target_pairs={{0,6},{1,7},{2,8},{3,9},{4,10},{5,11},{6,12},{7,13},{8,14},{9,15},... | collective-permute-start | bytes 61448
  1276.4 105.2 %collective-permute-start.6 = (bf16[24,2560]{1,0:T(8,128)(2,1)S(1)}, bf16[24,2560]{1,0:T(8,128)(2,1)S(1)}, u32[]{:S(2)}, u32[]{:S(2)}) collective-permute-start(bf16[24,2560]{1,0:T(8,128)(2,1)S(1)} %fusion.2), channel_id=1, source_target_pairs={{0,5},{1,6},{2,7},{3,8},{4,9},{5,10},{6,11},{7,12},{8,13},{9,14},{... | collective-permute-start | bytes 368648
  1277.7 103.9 %collective-permute-start.5 = (bf16[24,2560]{1,0:T(8,128)(2,1)S(1)}, bf16[24,2560]{1,0:T(8,128)(2,1)S(1)}, u32[]{:S(2)}, u32[]{:S(2)}) collective-permute-start(bf16[24,2560]{1,0:T(8,128)(2,1)S(1)} %fusion.2), channel_id=1, source_target_pairs={{0,4},{1,5},{2,6},{3,7},{4,8},{5,9},{6,10},{7,11},{8,12},{9,13},{1... | collective-permute-start | bytes 368648
  1283.8 97.9 %collective-permute-start.4 = (bf16[24,2560]{1,0:T(8,128)(2,1)S(1)}, bf16[24,2560]{1,0:T(8,128)(2,1)S(1)}, u32[]{:S(2)}, u32[]{:S(2)}) collective-permute-start(bf16[24,2560]{1,0:T(8,128)(2,1)S(1)} %fusion.2), channel_id=1, source_target_pairs={{0,3},{1,4},{2,5},{3,6},{4,7},{5,8},{6,9},{7,10},{8,11},{9,12},{10... | collective-permute-start | bytes 368648
  1288.4 93.3 %collective-permute-start.3 = (bf16[24,2560]{1,0:T(8,128)(2,1)S(1)}, bf16[24,2560]{1,0:T(8,128)(2,1)S(1)}, u32[]{:S(2)}, u32[]{:S(2)}) collective-permute-start(bf16[24,2560]{1,0:T(8,128)(2,1)S(1)} %fusion.2), channel_id=1, source_target_pairs={{0,2},{1,3},{2,4},{3,5},{4,6},{5,7},{6,8},{7,9},{8,10},{9,11},{10,... | collective-permute-start | bytes 368648
  1294.6 87.0 %collective-permute-start.2 = (bf16[24,2560]{1,0:T(8,128)(2,1)S(1)}, bf16[24,2560]{1,0:T(8,128)(2,1)S(1)}, u32[]{:S(2)}, u32[]{:S(2)}) collective-permute-start(bf16[24,2560]{1,0:T(8,128)(2,1)S(1)} %fusion.2), channel_id=1, source_target_pairs={{0,1},{1,2},{2,3},{3,4},{4,5},{5,6},{6,7},{7,8},{8,9},{9,10},{10,1... | collective-permute-start | bytes 368648
  (299 other events, 619.8 us)
Sparse Core Ops, SparseCore 0:
  11.2 93.1 all-gather.7
  107.0 73.6 all-gather.9
  1182.1 73.3 all-gather.11
  1259.2 196.3 reduce-scatter.3
